TPU v7x, 256 devices: a whole 4x4x8 slice. The times are simulated.
256 devices in a mesh: gx: 32 (over x, y, core), gy: 8 (over z).
Axes of the slice: x: 4, y: 4, z: 8, core: 2. Of those that a mesh axis runs over, the one named last changes fastest.
Arguments:
- tokens: bfloat16 [512, 16384], P('gy', 'gx'), may hold values from -6 to 6
- gate_weight: bfloat16 [16384, 26624], P('gx', 'gy'), may hold values from -0.046875 to 0.046875
- up_weight: bfloat16 [16384, 26624], P('gx', 'gy'), may hold values from -0.046875 to 0.046875
- down_weight: bfloat16 [26624, 16384], P('gy', 'gx'), may hold values from -0.0390625 to 0.0390625
Outputs:
- layer_out: bfloat16 [512, 16384], P('gy', 'gx')
All inputs are finite; a program needn't handle non-finite values.
Results may differ from a plain program's by a relative error of at most 0.0049.
Values may be sent and summed in bfloat16 or wider, within the bound.
A program may use at most 128 MiB of HBM per device.

v0:
```python
import jax
import jax.numpy as jnp
from jax import lax
from jax.sharding import PartitionSpec as P


def on_device(tokens, gate_weight, up_weight, down_weight):
    feats = lax.all_gather(tokens, "gy", axis=0, tiled=True)
    gate_part = jnp.dot(feats, gate_weight, preferred_element_type=jnp.float32)
    up_part = jnp.dot(feats, up_weight, preferred_element_type=jnp.float32)
    terms = jnp.stack((gate_part, up_part), axis=0)
    summed = lax.psum_scatter(terms, "gx", scatter_dimension=1, tiled=True)
    gate, up = (summed[0], summed[1])
    hidden = (jax.nn.silu(gate) * up).astype(jnp.bfloat16)
    partial_out = jnp.dot(
        lax.all_gather(hidden, "gx", axis=0, tiled=True),
        down_weight,
        preferred_element_type=jnp.float32,
    )
    return lax.psum_scatter(partial_out, "gy", scatter_dimension=0, tiled=True).astype(jnp.bfloat16)


def solution(mesh):
    return jax.shard_map(
        on_device,
        mesh=mesh,
        in_specs=(P("gy", "gx"), P("gx", "gy"), P("gx", "gy"), P("gy", "gx")),
        out_specs=P("gy", "gx"),
        check_vma=False,
    )
```

profile of v0, /device:TPU:1, one launch (start us, length us, event | category | flops | bytes accessed | tf_op | source)
XLA Modules:
  0.0 271.0 jit_solution(9852510709673941315)
XLA Ops:
  6.5 0.0 copy-start
  6.5 0.0 reduce-scatter.3.cloned.1.call-start
  6.5 24.1 %all_gather.6 = bf16[512,512]{1,0:T(8,128)(2,1)S(1)} all-gather(bf16[64,512]{1,0:T(8,128)(2,1)} %param.4), channel_id=1, replica_groups=mesh['gx'=32,'gy'=8] {'gy'}, dimensions={0}, use_global_device_ids=true | all-gather | bytes 589824 | tf_op jit(solution)/shard_map/all_gather | solution.py:8
  30.6 0.0 copy-done
  30.6 0.0 copy-start.1
  30.6 4.7 %convolution_bitcast_fusion = f32[1,512,3328]{2,1,0:T(8,128)} fusion(bf16[512,512]{1,0:T(8,128)(2,1)S(1)} %all_gather.6, bf16[512,3328]{1,0:T(8,128)(2,1)S(1)} %copy-done), kind=kOutput, calls=%fused_computation.1 | convolution fusion | flops 1744830464 | bytes 10747904 | tf_op jit(solution)/shard_map/dot_general | solution.py:10
  35.3 0.0 copy-done.1
  35.3 4.7 %convolution_bitcast_fusion.1 = f32[1,512,3328]{2,1,0:T(8,128)} fusion(bf16[512,512]{1,0:T(8,128)(2,1)S(1)} %all_gather.6, bf16[512,3328]{1,0:T(8,128)(2,1)S(1)} %copy-done.1), kind=kOutput, calls=%fused_computation.2 | convolution fusion | flops 1744830464 | bytes 10747904 | tf_op jit(solution)/shard_map/dot_general | solution.py:9
  40.0 10.6 %pad_maximum_fusion = f32[2,512,3328]{2,1,0:T(8,128)} fusion(f32[1,512,3328]{2,1,0:T(8,128)} %convolution_bitcast_fusion, f32[1,512,3328]{2,1,0:T(8,128)} %convolution_bitcast_fusion.1), kind=kLoop, calls=%fused_computation | loop fusion | flops 3407872 | bytes 27262976 | tf_op jit(solution)/shard_map/stack | solution.py:11
  50.7 0.0 reduce-scatter.3.cloned.1.call-update
  50.7 0.0 all-gather.2.cloned.1.call-start
  50.7 119.2 %reduce-scatter.3.cloned.1.call-done = f32[2,16,3328]{2,1,0:T(8,128)} async-done(((f32[2,512,3328]{2,1,0:T(8,128)}), f32[2,16,3328]{2,1,0:T(8,128)}) %reduce-scatter.3.cloned.1.call-update) | async-done | bytes 426000 | tf_op jit(solution)/shard_map/reduce_scatter | solution.py:12
  169.9 1.7 fusion.1
  171.7 0.0 all-gather.2.cloned.1.call-update
  171.7 0.0 reduce-scatter.5.cloned.1.call-start
  171.7 52.4 %all-gather.2.cloned.1.call-done = bf16[512,3328]{1,0:T(8,128)(2,1)} async-done(((bf16[16,3328]{1,0:T(8,128)(2,1)}), bf16[512,3328]{1,0:T(8,128)(2,1)}) %all-gather.2.cloned.1.call-update) | async-done | bytes 3407888 | tf_op jit(solution)/shard_map/all_gather | solution.py:16
  224.1 5.9 %fusion.2 = f32[512,512]{1,0:T(8,128)} fusion(bf16[512,3328]{1,0:T(8,128)(2,1)} %all-gather.2.cloned.1.call-done, bf16[3328,512]{1,0:T(8,128)(2,1)} %param.7), kind=kOutput, calls=%fused_computation.7 | convolution fusion | flops 1744830464 | bytes 7864320 | tf_op jit(solution)/shard_map/dot_general | solution.py:15
  230.0 0.0 reduce-scatter.5.cloned.1.call-update
  230.0 32.9 %reduce-scatter.5.cloned.1.call-done = f32[64,512]{1,0:T(8,128)} async-done(((f32[512,512]{1,0:T(8,128)}), f32[64,512]{1,0:T(8,128)}) %reduce-scatter.5.cloned.1.call-update) | async-done | bytes 131088 | tf_op jit(solution)/shard_map/reduce_scatter | solution.py:20
  263.0 1.5 convert_element_type.7
Async XLA Ops:
  6.5 24.1 %copy-start = (bf16[512,3328]{1,0:T(8,128)(2,1)S(1)}, bf16[512,3328]{1,0:T(8,128)(2,1)}, u32[]{:S(2)}) copy-start(bf16[512,3328]{1,0:T(8,128)(2,1)} %param.6) | copy-start | bytes 10223620
  6.5 163.4 %reduce-scatter.3.cloned.1.call-start = ((), (), s32[]{:S(2)}) async-start(), calls=%async_computation.2 | async-start | bytes 14057472 | tf_op jit(solution)/shard_map/reduce_scatter | solution.py:12
  30.6 4.7 %copy-start.1 = (bf16[512,3328]{1,0:T(8,128)(2,1)S(1)}, bf16[512,3328]{1,0:T(8,128)(2,1)}, u32[]{:S(2)}) copy-start(bf16[512,3328]{1,0:T(8,128)(2,1)} %param.5) | copy-start | bytes 10223620
  50.7 173.4 %all-gather.2.cloned.1.call-start = ((), (), s32[]{:S(2)}) async-start(), calls=%async_computation.3 | async-start | bytes 3514368 | tf_op jit(solution)/shard_map/all_gather | solution.py:16
  171.7 91.3 %reduce-scatter.5.cloned.1.call-start = ((), (), s32[]{:S(2)}) async-start(), calls=%async_computation.4 | async-start | bytes 1179648 | tf_op jit(solution)/shard_map/reduce_scatter | solution.py:20
Sparse Core Ops, SparseCore 0:
  50.8 119.0 reduce-scatter.2
  172.8 51.2 all-gather.1
  230.2 32.7 reduce-scatter.4
where the time goes:
time: 275 us; the launch traced here: 271 us
  waiting for transfers between devices  205 us (75%)
  blocking collectives  24.1 us (9%)
  matrix products  15.3 us (6%)
  other arithmetic  13.9 us (5%)
  between operations  13.1 us (5%)
    reduce_scatter x1, waiting for transfers between devices, on_device(): summed = lax.psum_scatter(terms, 'gx', scatter_dimension=1, tiled=True)  119 us
    all_gather x1, waiting for transfers between devices, on_device(): lax.all_gather(hidden, 'gx', axis=0, tiled=True)  52.4 us
    reduce_scatter x1, waiting for transfers between devices, on_device(): lax.psum_scatter(partial_out, 'gy', scatter_dimension=0, tiled=True)  32.9 us
    all_gather x1, blocking collectives, on_device(): feats = lax.all_gather(tokens, 'gy', axis=0, tiled=True)  24.1 us
    another operation x1, other arithmetic, on_device(): terms = jnp.stack((gate_part, up_part), axis=0)  10.6 us
    dot_general x1, matrix products, on_device(): jnp.dot(lax.all_gather(hidden, 'gx', axis=0, tiled=True), down_weight, pr...  5.9 us
  transfers between devices with their start and end apart: 3, of which 3 were waited for; matrix products, arithmetic and copies ran while one was open for 0% of the time, Pallas kernels for 0%

commit v1 on v0

v1 whole, which is shorter than its diff:
```python
import functools

import jax
import jax.numpy as jnp
from jax import lax
from jax.experimental import pallas as pl
from jax.experimental.pallas import tpu as pltpu
from jax.sharding import PartitionSpec as P

MESH = pl.DeviceIdType.MESH
GROUPS = 4
PIECES = (896, 768)
OWNERS = ((0, 7), (2, 5), (4, 3), (1, 6))
TILE = 256
LAGS = (0, 2, 4, 6, 8, 9)


def kernel(tok_hbm, gate_hbm, up_hbm, down_hbm, out_ref,
           wb, wd, tokc, pf, pb, r1, s2f, s2b, r2, hid, yf, yb, zr,
           loc_sem, w_ss, w_rs, t_ss, t_rs, f_ss, f_rs, s1_ss, s1_rs, s2_ss, s2_rs,
           g1_ss, g1_rs, g2_ss, g2_rs, sib_ss, sib_rs, z_ss, z_rs):
    gx = lax.axis_index("gx")
    z = lax.axis_index("gy")
    core = gx % 2
    y = (gx // 2) % 4
    x = gx // 8
    half = wb.shape[2] // 2
    cols = wb.shape[2]
    p = x * (1 - core) + y * core
    q = y * (1 - core) + x * core

    def device(x_, y_, core_, z_):
        return {"gx": (x_ % 4) * 8 + (y_ % 4) * 2 + core_, "gy": z_ % 8}

    def first(step):
        return device(x + step * (1 - core), y + step * core, core, z)

    def second(step):
        return device(x + step * core, y + step * (1 - core), core, z)

    def along_z(step):
        return device(x, y, core, z + step)

    sibling = device(x, y, 1 - core, z)

    def remote(src, dst, ss, rs, to):
        return pltpu.make_async_remote_copy(src_ref=src, dst_ref=dst, send_sem=ss, recv_sem=rs, device_id=to, device_id_type=MESH)

    sent = []

    def go(copy):
        copy.start()
        sent.append(copy)
        return copy

    rows = tok_hbm.shape[0]
    starts = [sum(PIECES[:h]) for h in range(len(PIECES))]
    slot = {o: (g, j) for g in range(GROUPS) for j, o in enumerate(OWNERS[g])}

    def tokens_at(o):
        g, j = slot[o]
        return tokc.at[g, core, pl.ds(j * rows, rows)]

    def weight_copies(owner, h, make):
        copies = []
        for i, hbm in enumerate((gate_hbm, up_hbm)):
            src = hbm.at[:, pl.ds(pl.multiple_of(owner * half + starts[h], 128), PIECES[h])]
            dst = wb.at[core, :, pl.ds(2 * starts[h] + i * PIECES[h], PIECES[h])]
            copies.append(make(src, dst, 2 * h + i))
        return copies

    own_tokens = pltpu.make_async_copy(tok_hbm, tokens_at(0), loc_sem.at[0])
    own_tokens.start()
    own_weights = [weight_copies(core, h, lambda src, dst, i: pltpu.make_async_copy(src, dst, loc_sem.at[2 + i])) for h in range(2)]
    own_down = pltpu.make_async_copy(down_hbm, wd, loc_sem.at[1])
    for copy in own_weights[0]:
        copy.start()

    barrier = pltpu.get_barrier_semaphore()
    peers = [sibling, first(1), first(2), first(3), second(1), second(2), second(3)] + [along_z(s) for s in range(1, 8)]
    for peer in peers:
        pl.semaphore_signal(barrier, inc=1, device_id=peer, device_id_type=MESH)
    pl.semaphore_wait(barrier, len(peers))

    def swap_weights(h):
        return weight_copies(1 - core, h, lambda src, dst, i: go(remote(src, dst, w_ss.at[i], w_rs.at[i], sibling)))

    def pass_tokens(src, o, step):
        return go(remote(src, tokens_at(o), t_ss.at[o], t_rs.at[o], along_z(step)))

    def share_tokens(o):
        return go(remote(tokens_at(o), tokens_at(o), f_ss.at[o], f_rs.at[o], sibling))

    arrive = {1: pass_tokens(tok_hbm, 1, 7), 7: pass_tokens(tok_hbm, 7, 1)}
    swapped = [swap_weights(0)]
    for h in range(1, len(PIECES)):
        for copy in own_weights[h]:
            copy.start()
    own_down.start()
    own_tokens.wait()
    shared = {0: share_tokens(0)}

    def relay(distance):
        for o in (distance, 8 - distance)[:1 if distance == 4 else 2]:
            arrive[o].wait_recv()
            shared[o] = share_tokens(o)
            if o < 4:
                arrive[o + 1] = pass_tokens(tokens_at(o), o + 1, 7)
            elif o > 5:
                arrive[o - 1] = pass_tokens(tokens_at(o), o - 1, 1)

    def weights_ready(h):
        for copy in own_weights[h]:
            copy.wait()
        for copy in swapped[h]:
            copy.wait_recv()

    def span(h, width=2):
        return pl.ds(width * starts[h], width * PIECES[h])

    def over_tiles(h, body):
        @pl.loop(0, 2 * PIECES[h] // TILE)
        def _(n):
            body(pl.ds(pl.multiple_of(2 * starts[h] + n * TILE, TILE), TILE))

    s1, s2, g1, g2, sib = {}, {}, {}, {}, {}
    zs = {}

    def scatter(c, src, dst, ss, rs, to):
        i = 2 * c[0] + c[1]
        return [go(remote(src(d), dst(d), ss.at[i, d - 1], rs.at[i, d - 1], to(d))) for d in (2, 1, 3)]

    def stage_m(c):
        g, h = c
        if h == 0:
            for o in OWNERS[g]:
                shared[o].wait_recv()

        def body(at):
            acc = jnp.dot(tokc[g, 0], wb[0, :, at], preferred_element_type=jnp.float32)
            acc += jnp.dot(tokc[g, 1], wb[1, :, at], preferred_element_type=jnp.float32)
            pf[g, :, :, at] = acc.reshape(4, 32, TILE)
            pb[g, :, :, at] = acc.astype(jnp.bfloat16).reshape(4, 32, TILE)

        over_tiles(h, body)
        s1[c] = scatter(c, lambda d: pb.at[g, (p + d) % 4, :, span(h)], lambda d: r1.at[g, d - 1, :, span(h)], s1_ss, s1_rs, first)

    def stage_1(c):
        g, h = c
        for copy in s1[c]:
            copy.wait_recv()

        def body(at):
            acc = pf[g, p, :, at]
            for d in range(3):
                acc += r1[g, d, :, at].astype(jnp.float32)
            acc = acc.reshape(4, 8, TILE)
            s2f[g, :, :, at] = acc
            s2b[g, :, :, at] = acc.astype(jnp.bfloat16)

        over_tiles(h, body)
        s2[c] = scatter(c, lambda d: s2b.at[g, (q + d) % 4, :, span(h)], lambda d: r2.at[g, d - 1, :, span(h)], s2_ss, s2_rs, second)

    def stage_2(c):
        g, h = c
        for copy in s2[c]:
            copy.wait_recv()
        acc = s2f[g, q, :, span(h)]
        for d in range(3):
            acc += r2[g, d, :, span(h)].astype(jnp.float32)
        gate, up = acc[:, :PIECES[h]], acc[:, PIECES[h]:]
        hid[core, g, p * 4 + q, :, span(h, 1)] = (gate / (1.0 + jnp.exp(-gate)) * up).astype(jnp.bfloat16)
        place = hid.at[core, g, p * 4 + q, :, span(h, 1)]
        g1[c] = scatter(c, lambda d: place, lambda d: place, g1_ss, g1_rs, second)

    def stage_3(c):
        g, h = c
        for copy in g1[c]:
            copy.wait_recv()
        place = hid.at[core, g, pl.ds(p * 4, 4), :, span(h, 1)]
        g2[c] = scatter(c, lambda d: place, lambda d: place, g2_ss, g2_rs, first)

    def stage_4(c):
        g, h = c
        for copy in g2[c]:
            copy.wait_recv()
        place = hid.at[core, g, :, :, span(h, 1)]
        sib[c] = go(remote(place, place, sib_ss.at[2 * g + h], sib_rs.at[2 * g + h], sibling))

    def stage_5(c):
        g, h = c
        if h != len(PIECES) - 1:
            return
        for h in range(len(PIECES)):
            sib[g, h].wait_recv()
        if g == 0:
            own_down.wait()
        acc = None
        for i in range(2):
            units = hid[i, g].astype(jnp.float32).reshape(128, half).astype(jnp.bfloat16)
            term = jnp.dot(units, wd[pl.ds(i * half, half), :], preferred_element_type=jnp.float32)
            acc = term if acc is None else acc + term
        for j in range(2):
            o = OWNERS[g][j]
            part = acc[j * rows:(j + 1) * rows]
            if o == 0:
                yf[...] = part
            else:
                yb[o] = part.astype(jnp.bfloat16)
                zs[o] = go(remote(yb.at[o], zr.at[o], z_ss.at[o], z_rs.at[o], along_z(o)))

    chunks = [(g, h) for g in range(GROUPS) for h in range(len(PIECES))]
    stages = (stage_m, stage_1, stage_2, stage_3, stage_4, stage_5)
    relay(1)
    weights_ready(0)
    swapped.append(swap_weights(1))
    for t in range(len(chunks) + LAGS[-1]):
        for stage, lag in zip(stages, LAGS):
            if 0 <= t - lag < len(chunks):
                stage(chunks[t - lag])
        if t < 3:
            relay(t + 2)
        if t == 0:
            weights_ready(1)

    total = yf[...]
    for g in range(GROUPS):
        for o in OWNERS[g]:
            if o:
                zs[o].wait_recv()
                total += zr[o].astype(jnp.float32)
    out_ref[...] = total.astype(jnp.bfloat16)
    for copy in sent:
        copy.wait_send()


def on_device(tokens, gate_weight, up_weight, down_weight):
    rows, depth = tokens.shape
    hidden = gate_weight.shape[1]
    half = hidden // 2
    bf16, f32 = jnp.bfloat16, jnp.float32
    dma = pltpu.SemaphoreType.DMA
    n = GROUPS
    m = 2 * n
    return pl.pallas_call(
        kernel,
        out_shape=jax.ShapeDtypeStruct((rows, down_weight.shape[1]), bf16),
        in_specs=[pl.BlockSpec(memory_space=pl.ANY)] * 4,
        out_specs=pl.BlockSpec(memory_space=pltpu.VMEM),
        scratch_shapes=[
            pltpu.VMEM((2, depth, hidden), bf16),
            pltpu.VMEM(down_weight.shape, bf16),
            pltpu.VMEM((n, 2, 2 * rows, depth), bf16),
            pltpu.VMEM((n, 4, 32, hidden), f32),
            pltpu.VMEM((n, 4, 32, hidden), bf16),
            pltpu.VMEM((n, 3, 32, hidden), bf16),
            pltpu.VMEM((n, 4, 8, hidden), f32),
            pltpu.VMEM((n, 4, 8, hidden), bf16),
            pltpu.VMEM((n, 3, 8, hidden), bf16),
            pltpu.VMEM((2, n, 16, 8, half), bf16),
            pltpu.VMEM((rows, down_weight.shape[1]), f32),
            pltpu.VMEM((8, rows, down_weight.shape[1]), bf16),
            pltpu.VMEM((8, rows, down_weight.shape[1]), bf16),
            dma((6,)), dma((4,)), dma((4,)),
            dma((8,)), dma((8,)), dma((8,)), dma((8,)),
            dma((m, 3)), dma((m, 3)), dma((m, 3)), dma((m, 3)),
            dma((m, 3)), dma((m, 3)), dma((m, 3)), dma((m, 3)),
            dma((m,)), dma((m,)), dma((8,)), dma((8,)),
        ],
        compiler_params=pltpu.CompilerParams(collective_id=0, has_side_effects=True, vmem_limit_bytes=56 << 20),
    )(tokens, gate_weight, up_weight, down_weight)


def solution(mesh):
    return jax.shard_map(
        on_device,
        mesh=mesh,
        in_specs=(P("gy", "gx"), P("gx", "gy"), P("gx", "gy"), P("gy", "gx")),
        out_specs=P("gy", "gx"),
        check_vma=False,
    )
```

time: 275 us -> 73 us (0.27); the launches traced: 271 us -> 72.9 us
  waiting for transfers between devices: 205 us -> 0 us
  Pallas kernels: 0 us -> 71.4 us
  blocking collectives: 24.1 us -> 0 us
  matrix products: 15.3 us -> 0 us
  other arithmetic: 13.9 us -> 0 us
  between operations: 13.1 us -> 0.01 us
    reduce_scatter x2 -> x0, waiting for transfers between devices: 152 us -> none  [the longest x1 119 us: on_device(): summed = lax.psum_scatter(terms, 'gx', scatter_dimension=1, tiled=True)]
    pallas_call x0 -> x1, Pallas kernels: none -> 71.4 us  [on_device(): pl.pallas_call(kernel, out_shape=jax.ShapeDtypeStruct((rows, down_weight....]
    all_gather x1 -> x0, waiting for transfers between devices: 52.4 us -> none  [on_device(): lax.all_gather(hidden, 'gx', axis=0, tiled=True)]
    all_gather x1 -> x0, blocking collectives: 24.1 us -> none  [on_device(): feats = lax.all_gather(tokens, 'gy', axis=0, tiled=True)]
    dot_general x3 -> x0, matrix products: 15.3 us -> none  [the longest x1 5.9 us: on_device(): jnp.dot(lax.all_gather(hidden, 'gx', axis=0, tiled=True), down_weight, pr...]
    another operation x1 -> x0, other arithmetic: 10.6 us -> none  [on_device(): terms = jnp.stack((gate_part, up_part), axis=0)]
    convert_element_type x2 -> x0, other arithmetic: 3.28 us -> none  [the longest x1 1.74 us: on_device(): hidden = (jax.nn.silu(gate) * up).astype(jnp.bfloat16)]
  transfers between devices with their start and end apart: 3 -> 0, of which waited for: 3 -> 0; matrix products, arithmetic and copies ran while one was open for 0% -> 0% of each run, Pallas kernels for 0% -> 0%
where the time goes in v1:
time: 73 us; the launch traced here: 72.9 us
  Pallas kernels  71.4 us (98%)
  local copies, waits for them, and re-layouts  1.47 us (2%)
    pallas_call x1, Pallas kernels, on_device(): pl.pallas_call(kernel, out_shape=jax.ShapeDtypeStruct((rows, down_weight....  71.4 us
    unnamed x1, local copies, waits for them, and re-layouts  1.47 us

profile of v1, /device:TPU:1, one launch (start us, length us, event | category | flops | bytes accessed | tf_op | source)
XLA Modules:
  0.0 72.9 jit_solution(15098302543552086907)
XLA Ops:
  0.0 71.4 %shard_map.46 = bf16[64,512]{1,0:T(8,128)(2,1)} custom-call(bf16[64,512]{1,0:T(8,128)(2,1)} %tok_hbm.1, bf16[512,3328]{1,0:T(8,128)(2,1)} %gate_hbm.1, bf16[512,3328]{1,0:T(8,128)(2,1)} %up_hbm.1, bf16[3328,512]{1,0:T(8,128)(2,1)} %down_hbm.1), custom_call_target="tpu_custom_call" | custom-call | tf_op jit(solution)/shard_map/pallas_call | solution.py:245
  71.5 1.5 %copy.6 = bf16[64,512]{1,0:T(8,128)(2,1)} copy(bf16[64,512]{1,0:T(8,128)(2,1)} %shard_map.46) | data formatting | bytes 131072

commit v2 on v1

--- a/solution.py
+++ b/solution.py
@@ -10,13 +10,14 @@
 MESH = pl.DeviceIdType.MESH
 GROUPS = 4
 PIECES = (896, 768)
-OWNERS = ((0, 7), (2, 5), (4, 3), (1, 6))
+OWNERS = ((0, 7), (2, 5), (4, 3), (6, 1))
 TILE = 256
 LAGS = (0, 2, 4, 6, 8, 9)
+RELAYS = {0: 2, 1: 3, 3: 4}
 
 
 def kernel(tok_hbm, gate_hbm, up_hbm, down_hbm, out_ref,
-           wb, wd, tokc, pf, pb, r1, s2f, s2b, r2, hid, yf, yb, zr,
+           wb, wd, tokc, pf, pb, r1, s2f, s2b, r2, hid, ya, yb, zr,
            loc_sem, w_ss, w_rs, t_ss, t_rs, f_ss, f_rs, s1_ss, s1_rs, s2_ss, s2_rs,
            g1_ss, g1_rs, g2_ss, g2_rs, sib_ss, sib_rs, z_ss, z_rs):
     gx = lax.axis_index("gx")
@@ -77,7 +78,7 @@
         copy.start()
 
     barrier = pltpu.get_barrier_semaphore()
-    peers = [sibling, first(1), first(2), first(3), second(1), second(2), second(3)] + [along_z(s) for s in range(1, 8)]
+    peers = [sibling, first(1), first(2), first(3), second(1), second(2), second(3)] + [along_z(s) for s in (1, 7)]
     for peer in peers:
         pl.semaphore_signal(barrier, inc=1, device_id=peer, device_id_type=MESH)
     pl.semaphore_wait(barrier, len(peers))
@@ -126,9 +127,13 @@
     s1, s2, g1, g2, sib = {}, {}, {}, {}, {}
     zs = {}
 
-    def scatter(c, src, dst, ss, rs, to):
+    def scatter(c, src, dst, landing, ss, rs, to):
         i = 2 * c[0] + c[1]
-        return [go(remote(src(d), dst(d), ss.at[i, d - 1], rs.at[i, d - 1], to(d))) for d in (2, 1, 3)]
+        for d in (2, 1, 3):
+            remote(src(d), dst(d), ss.at[i], rs.at[i], to(d)).start()
+        three = remote(landing, landing, ss.at[i], rs.at[i], to(1))
+        sent.append(three)
+        return three
 
     def stage_m(c):
         g, h = c
@@ -143,12 +148,11 @@
             pb[g, :, :, at] = acc.astype(jnp.bfloat16).reshape(4, 32, TILE)
 
         over_tiles(h, body)
-        s1[c] = scatter(c, lambda d: pb.at[g, (p + d) % 4, :, span(h)], lambda d: r1.at[g, d - 1, :, span(h)], s1_ss, s1_rs, first)
+        s1[c] = scatter(c, lambda d: pb.at[g, (p + d) % 4, :, span(h)], lambda d: r1.at[g, d - 1, :, span(h)], r1.at[g, :, :, span(h)], s1_ss, s1_rs, first)
 
     def stage_1(c):
         g, h = c
-        for copy in s1[c]:
-            copy.wait_recv()
+        s1[c].wait_recv()
 
         def body(at):
             acc = pf[g, p, :, at]
@@ -159,52 +163,46 @@
             s2b[g, :, :, at] = acc.astype(jnp.bfloat16)
 
         over_tiles(h, body)
-        s2[c] = scatter(c, lambda d: s2b.at[g, (q + d) % 4, :, span(h)], lambda d: r2.at[g, d - 1, :, span(h)], s2_ss, s2_rs, second)
+        s2[c] = scatter(c, lambda d: s2b.at[g, (q + d) % 4, :, span(h)], lambda d: r2.at[g, d - 1, :, span(h)], r2.at[g, :, :, span(h)], s2_ss, s2_rs, second)
 
     def stage_2(c):
         g, h = c
-        for copy in s2[c]:
-            copy.wait_recv()
+        s2[c].wait_recv()
         acc = s2f[g, q, :, span(h)]
         for d in range(3):
             acc += r2[g, d, :, span(h)].astype(jnp.float32)
         gate, up = acc[:, :PIECES[h]], acc[:, PIECES[h]:]
         hid[core, g, p * 4 + q, :, span(h, 1)] = (gate / (1.0 + jnp.exp(-gate)) * up).astype(jnp.bfloat16)
         place = hid.at[core, g, p * 4 + q, :, span(h, 1)]
-        g1[c] = scatter(c, lambda d: place, lambda d: place, g1_ss, g1_rs, second)
+        g1[c] = scatter(c, lambda d: place, lambda d: place, hid.at[core, g, pl.ds(0, 3), :, span(h, 1)], g1_ss, g1_rs, second)
 
     def stage_3(c):
         g, h = c
-        for copy in g1[c]:
-            copy.wait_recv()
+        g1[c].wait_recv()
         place = hid.at[core, g, pl.ds(p * 4, 4), :, span(h, 1)]
-        g2[c] = scatter(c, lambda d: place, lambda d: place, g2_ss, g2_rs, first)
+        g2[c] = scatter(c, lambda d: place, lambda d: place, hid.at[core, g, pl.ds(0, 12), :, span(h, 1)], g2_ss, g2_rs, first)
 
     def stage_4(c):
         g, h = c
-        for copy in g2[c]:
-            copy.wait_recv()
+        g2[c].wait_recv()
         place = hid.at[core, g, :, :, span(h, 1)]
         sib[c] = go(remote(place, place, sib_ss.at[2 * g + h], sib_rs.at[2 * g + h], sibling))
 
     def stage_5(c):
         g, h = c
-        if h != len(PIECES) - 1:
-            return
-        for h in range(len(PIECES)):
-            sib[g, h].wait_recv()
-        if g == 0:
+        sib[c].wait_recv()
+        if c == (0, 0):
             own_down.wait()
-        acc = None
-        for i in range(2):
-            units = hid[i, g].astype(jnp.float32).reshape(128, half).astype(jnp.bfloat16)
-            term = jnp.dot(units, wd[pl.ds(i * half, half), :], preferred_element_type=jnp.float32)
-            acc = term if acc is None else acc + term
+        last = h == len(PIECES) - 1
         for j in range(2):
             o = OWNERS[g][j]
-            part = acc[j * rows:(j + 1) * rows]
-            if o == 0:
-                yf[...] = part
+            part = None if h == 0 else ya[g, j]
+            for i in range(2):
+                units = hid[i, g, pl.ds(8 * j, 8), :, span(h, 1)].astype(jnp.float32).reshape(rows, PIECES[h]).astype(jnp.bfloat16)
+                term = jnp.dot(units, wd[pl.ds(i * half + starts[h], PIECES[h]), :], preferred_element_type=jnp.float32)
+                part = term if part is None else part + term
+            if not last or o == 0:
+                ya[g, j] = part
             else:
                 yb[o] = part.astype(jnp.bfloat16)
                 zs[o] = go(remote(yb.at[o], zr.at[o], z_ss.at[o], z_rs.at[o], along_z(o)))
@@ -218,20 +216,20 @@
         for stage, lag in zip(stages, LAGS):
             if 0 <= t - lag < len(chunks):
                 stage(chunks[t - lag])
-        if t < 3:
-            relay(t + 2)
+        if t in RELAYS:
+            relay(RELAYS[t])
         if t == 0:
             weights_ready(1)
 
-    total = yf[...]
+    for copy in sent:
+        copy.wait_send()
+    total = ya[0, 0]
     for g in range(GROUPS):
         for o in OWNERS[g]:
             if o:
                 zs[o].wait_recv()
                 total += zr[o].astype(jnp.float32)
     out_ref[...] = total.astype(jnp.bfloat16)
-    for copy in sent:
-        copy.wait_send()
 
 
 def on_device(tokens, gate_weight, up_weight, down_weight):
@@ -258,13 +256,13 @@
             pltpu.VMEM((n, 4, 8, hidden), bf16),
             pltpu.VMEM((n, 3, 8, hidden), bf16),
             pltpu.VMEM((2, n, 16, 8, half), bf16),
-            pltpu.VMEM((rows, down_weight.shape[1]), f32),
+            pltpu.VMEM((n, 2, rows, down_weight.shape[1]), f32),
             pltpu.VMEM((8, rows, down_weight.shape[1]), bf16),
             pltpu.VMEM((8, rows, down_weight.shape[1]), bf16),
             dma((6,)), dma((4,)), dma((4,)),
             dma((8,)), dma((8,)), dma((8,)), dma((8,)),
-            dma((m, 3)), dma((m, 3)), dma((m, 3)), dma((m, 3)),
-            dma((m, 3)), dma((m, 3)), dma((m, 3)), dma((m, 3)),
+            dma((m,)), dma((m,)), dma((m,)), dma((m,)),
+            dma((m,)), dma((m,)), dma((m,)), dma((m,)),
             dma((m,)), dma((m,)), dma((8,)), dma((8,)),
         ],
         compiler_params=pltpu.CompilerParams(collective_id=0, has_side_effects=True, vmem_limit_bytes=56 << 20),

time: 73 us -> 70.9 us (0.971)
  Pallas kernels: 71.4 us -> 69.3 us
    pallas_call x1, Pallas kernels: 71.4 us -> 69.3 us  [on_device(): pl.pallas_call(kernel, out_shape=jax.ShapeDtypeStruct((rows, down_weight....]
where the time goes in v2:
time: 70.9 us; the launch traced here: 70.8 us
  Pallas kernels  69.3 us (98%)
  local copies, waits for them, and re-layouts  1.47 us (2%)
    pallas_call x1, Pallas kernels, on_device(): pl.pallas_call(kernel, out_shape=jax.ShapeDtypeStruct((rows, down_weight....  69.3 us
    unnamed x1, local copies, waits for them, and re-layouts  1.47 us

profile of v2, /device:TPU:1, one launch (start us, length us, event | category | flops | bytes accessed | tf_op | source)
XLA Modules:
  0.0 70.8 jit_solution(11466435454213518322)
XLA Ops:
  0.0 69.3 %shard_map.46 = bf16[64,512]{1,0:T(8,128)(2,1)} custom-call(bf16[64,512]{1,0:T(8,128)(2,1)} %tok_hbm.1, bf16[512,3328]{1,0:T(8,128)(2,1)} %gate_hbm.1, bf16[512,3328]{1,0:T(8,128)(2,1)} %up_hbm.1, bf16[3328,512]{1,0:T(8,128)(2,1)} %down_hbm.1), custom_call_target="tpu_custom_call" | custom-call | tf_op jit(solution)/shard_map/pallas_call | solution.py:243
  69.3 1.5 %copy.6 = bf16[64,512]{1,0:T(8,128)(2,1)} copy(bf16[64,512]{1,0:T(8,128)(2,1)} %shard_map.46) | data formatting | bytes 131072

commit v3 on v2

--- a/solution.py
+++ b/solution.py
@@ -119,8 +119,8 @@
     def span(h, width=2):
         return pl.ds(width * starts[h], width * PIECES[h])
 
-    def over_tiles(h, body):
-        @pl.loop(0, 2 * PIECES[h] // TILE)
+    def over_tiles(h, body, unroll=False):
+        @pl.loop(0, 2 * PIECES[h] // TILE, unroll=unroll)
         def _(n):
             body(pl.ds(pl.multiple_of(2 * starts[h] + n * TILE, TILE), TILE))
 
@@ -147,7 +147,7 @@
             pf[g, :, :, at] = acc.reshape(4, 32, TILE)
             pb[g, :, :, at] = acc.astype(jnp.bfloat16).reshape(4, 32, TILE)
 
-        over_tiles(h, body)
+        over_tiles(h, body, unroll=True)
         s1[c] = scatter(c, lambda d: pb.at[g, (p + d) % 4, :, span(h)], lambda d: r1.at[g, d - 1, :, span(h)], r1.at[g, :, :, span(h)], s1_ss, s1_rs, first)
 
     def stage_1(c):

time: 70.9 us -> 69.6 us (0.982)
  Pallas kernels: 69.3 us -> 68 us
    pallas_call x1, Pallas kernels: 69.3 us -> 68 us  [on_device(): pl.pallas_call(kernel, out_shape=jax.ShapeDtypeStruct((rows, down_weight....]
where the time goes in v3:
time: 69.6 us; the launch traced here: 69.5 us
  Pallas kernels  68 us (98%)
  local copies, waits for them, and re-layouts  1.47 us (2%)
    pallas_call x1, Pallas kernels, on_device(): pl.pallas_call(kernel, out_shape=jax.ShapeDtypeStruct((rows, down_weight....  68 us
    unnamed x1, local copies, waits for them, and re-layouts  1.47 us

profile of v3, /device:TPU:1, one launch (start us, length us, event | category | flops | bytes accessed | tf_op | source)
XLA Modules:
  0.0 69.5 jit_solution(1363439604001879449)
XLA Ops:
  0.0 68.0 %shard_map.46 = bf16[64,512]{1,0:T(8,128)(2,1)} custom-call(bf16[64,512]{1,0:T(8,128)(2,1)} %tok_hbm.1, bf16[512,3328]{1,0:T(8,128)(2,1)} %gate_hbm.1, bf16[512,3328]{1,0:T(8,128)(2,1)} %up_hbm.1, bf16[3328,512]{1,0:T(8,128)(2,1)} %down_hbm.1), custom_call_target="tpu_custom_call" | custom-call | tf_op jit(solution)/shard_map/pallas_call | solution.py:243
  68.0 1.5 %copy.6 = bf16[64,512]{1,0:T(8,128)(2,1)} copy(bf16[64,512]{1,0:T(8,128)(2,1)} %shard_map.46) | data formatting | bytes 131072
